TPU v7x, 256 devices: a whole 4x4x8 slice. The times are simulated.
256 devices in a mesh: expert: 8 (over y, core), dp: 32 (over x, z).
Axes of the slice: x: 4, y: 4, z: 8, core: 2. Of those that a mesh axis runs over, the one named last changes fastest.
Arguments:
- hidden: bfloat16 [8, 14336, 1024], P('expert', 'dp'), may hold values from -6 to 6
- weight_codes: int32 [8, 14336, 2048], P('expert', 'dp'), may hold values from -8 to 7
- group_scales: float32 [8, 448, 2048], P('expert', 'dp'), may hold values from 0.0006681531 to 0.0050111483
- expert_index: int32 [4096, 2], P('expert'), may hold values from 0 to 7, all different within a row
- gate_values: float32 [4096, 2], P('expert'), may hold values from 0.2 to 1
- output_grad: bfloat16 [4096, 2048], P('expert', 'dp'), may hold values from -6 to 6
Outputs:
- combined: bfloat16 [4096, 2048], P('expert', 'dp')
- gate_grad: float32 [4096, 2], P('expert')
- hidden_grad: bfloat16 [8, 14336, 1024], P('expert', 'dp')
- weight_grad: float32 [8, 14336, 2048], P('expert', 'dp')
- scale_grad: float32 [8, 448, 2048], P('expert', 'dp')
Inputs may be any that keep to these rules, and one draw needn't show every extreme that they name: `expert_index`: the 2 entries of a token name different experts.
All inputs are finite; a program needn't handle non-finite values.
Results may differ from a plain program's by a relative error of at most 0.0058.
Values may be sent and summed in bfloat16 or wider, within the bound.
No kernel may reach another device: no remote copies, remote signals or barrier semaphores. Data moves between devices by JAX's collectives and lax.ppermute only.
A program may use at most 128 MiB of HBM per device.

v0:
```python
import jax
import jax.numpy as jnp
from jax import lax
from jax.sharding import PartitionSpec as P

EXPERTS = 8
GROUP = 32


def dequantize(weight_codes, group_scales):
    experts_here, units_here, feature_width = weight_codes.shape
    grouped = weight_codes.astype(jnp.float32).reshape(
        experts_here, units_here // GROUP, GROUP, feature_width
    )
    return (
        (grouped * group_scales[:, :, None, :])
        .reshape(experts_here, units_here, feature_width)
        .astype(jnp.bfloat16)
    )


def choice_ranks(flat_experts):
    onehot = (flat_experts[:, None] == jnp.arange(EXPERTS, dtype=jnp.int32)[None, :]).astype(
        jnp.int32
    )
    return jnp.sum((jnp.cumsum(onehot, axis=0) - onehot) * onehot, axis=1)


def on_device(hidden, weight_codes, group_scales, expert_index, gate_values, output_grad):
    local_experts = hidden.shape[0]
    slot_total = hidden.shape[2]
    feature_width = weight_codes.shape[2]
    expert_groups = lax.axis_size("expert")
    data_ranks = lax.axis_size("dp")
    tokens_here, choices = expert_index.shape
    capacity = tokens_here * choices // EXPERTS
    column_count = feature_width // data_ranks
    weight_table = dequantize(weight_codes, group_scales)
    table_cols = weight_table
    partial_value = jnp.einsum(
        "efs,efd->des", hidden, table_cols, preferred_element_type=jnp.float32
    )
    summed = lax.psum(partial_value.reshape(feature_width, local_experts * slot_total), "dp")
    owned_rows = lax.dynamic_slice_in_dim(
        summed, lax.axis_index("dp") * column_count, column_count, 0
    )
    outgoing = owned_rows.astype(jnp.bfloat16).reshape(column_count, local_experts, slot_total)
    returned = lax.all_to_all(outgoing, "expert", split_axis=2, concat_axis=2, tiled=True)
    returned = returned.reshape(column_count, local_experts * slot_total)
    flat_experts = expert_index.reshape(-1)
    ranking = choice_ranks(flat_experts)
    kept_mask = ranking < capacity
    clipped = jnp.minimum(ranking, capacity - 1)
    group_of = flat_experts // local_experts
    within = flat_experts % local_experts
    columns = jnp.arange(EXPERTS * capacity, dtype=jnp.int32)
    place_index = (within * expert_groups + group_of) * capacity + clipped
    picker = ((place_index[:, None] == columns[None, :]) & kept_mask[:, None]).astype(jnp.bfloat16)
    gathered = jnp.einsum("ac,dc->ad", picker, returned, preferred_element_type=jnp.float32)
    gathered = gathered.reshape(tokens_here, choices, column_count)
    keep_float = kept_mask.reshape(tokens_here, choices).astype(jnp.float32)
    weighted = gate_values * keep_float
    grad_float = output_grad.astype(jnp.float32)
    combined = jnp.sum(weighted[:, :, None] * gathered, axis=1).astype(jnp.bfloat16)
    gate_partial = keep_float * jnp.sum(grad_float[:, None, :] * gathered, axis=2)
    gate_grad = lax.psum(gate_partial, "dp")
    values = (
        (weighted[:, :, None] * grad_float[:, None, :])
        .reshape(tokens_here * choices, column_count)
        .astype(jnp.bfloat16)
    )
    outbound = jnp.einsum("ac,ad->cd", picker, values, preferred_element_type=jnp.float32).astype(
        jnp.bfloat16
    )
    outbound = outbound.reshape(local_experts, slot_total, column_count)
    arrived = lax.all_to_all(outbound, "expert", split_axis=1, concat_axis=1, tiled=True)
    block_cols = lax.all_gather(arrived, "dp", axis=2, tiled=True)
    table_cols = weight_table
    hidden_acc = jnp.einsum(
        "esd,efd->efs", block_cols, table_cols, preferred_element_type=jnp.float32
    )
    weight_piece = jnp.einsum(
        "efs,esd->efd", hidden, block_cols, preferred_element_type=jnp.float32
    )
    hidden_acc, weight_grad = (hidden_acc, weight_piece)
    hidden_grad = hidden_acc.astype(jnp.bfloat16)
    products = weight_grad * weight_codes.astype(jnp.float32)
    scale_grad = jnp.sum(products.reshape(local_experts, -1, GROUP, feature_width), axis=2)
    return (combined, gate_grad, hidden_grad, weight_grad, scale_grad)


def solution(mesh):
    return jax.shard_map(
        on_device,
        mesh=mesh,
        in_specs=(
            P("expert", "dp", None),
            P("expert", "dp", None),
            P("expert", "dp", None),
            P("expert", None),
            P("expert", None),
            P("expert", "dp"),
        ),
        out_specs=(
            P("expert", "dp"),
            P("expert", None),
            P("expert", "dp", None),
            P("expert", "dp", None),
            P("expert", "dp", None),
        ),
        check_vma=False,
    )
```

profile of v0, /device:TPU:8, one launch (start us, length us, event | category | flops | bytes accessed | tf_op | source)
XLA Modules:
  0.0 422.4 jit_solution(741626494181359657)
XLA Ops:
  7.2 0.9 copy.63
  8.5 2.3 reduce-window.6
  11.7 0.7 broadcast_select_fusion.1
  12.8 1.0 copy.77
  14.0 1.2 fusion.29
  16.1 2.3 reduce.3
  18.6 9.4 %all_to_all.10 = bf16[8,2,4096]{2,1,0:T(2,128)(2,1)S(1)} all-to-all(bf16[8,2,4096]{2,1,0:T(2,128)(2,1)S(1)} %reshape.142), channel_id=1, replica_groups=mesh['expert'=8,'dp'=32] {'expert'}, dimensions={0} | all-to-all | bytes 262144 | tf_op jit(solution)/shard_map/all_to_all | solution.py:76
  28.4 0.9 copy.74
  29.3 0.6 convert_element_type.45
  30.4 82.7 %all-gather.2.cloned.1.call-done = bf16[1,1024,2048]{1,2,0:T(8,128)(2,1)} async-done(((bf16[1,1024,64]{1,2,0:T(8,128)(2,1)}), bf16[1,1024,2048]{1,2,0:T(8,128)(2,1)}) %all-gather.2.cloned.1.call-update) | async-done | bytes 4194320 | tf_op jit(solution)/shard_map/all_gather | solution.py:77
  113.1 4.3 %fusion.12 = f32[1,448,2048]{2,1,0:T(8,128)S(1)} fusion(bf16[1,1024,2048]{1,2,0:T(8,128)(2,1)} %all-gather.2.cloned.1.call-done, bf16[1,448,1024]{2,1,0:T(8,128)(2,1)S(1)} %copy-done), kind=kOutput, calls=%fused_computation.14 | convolution fusion | flops 1879048192 | bytes 8781824 | tf_op jit(solution)/shard_map/efs,esd->efd/dot_general | solution.py:82
  117.8 2.9 copy-done.1
  120.7 3.1 convert_multiply_fusion
  123.9 5.6 %fusion.33 = f32[2048,1024]{1,0:T(8,128)} fusion(bf16[448,2048]{1,0:T(8,128)(2,1)S(1)} %get-tuple-element.13, bf16[1,448,1024]{2,1,0:T(8,128)(2,1)S(1)} %copy-done), kind=kOutput, calls=%fused_computation.25 | convolution fusion | flops 1879048192 | bytes 11141120 | tf_op jit(solution)/shard_map/efs,efd->des/dot_general | solution.py:40
  129.5 192.6 %all-reduce.1 = bf16[2048,1024]{1,0:T(8,128)(2,1)} all-reduce(f32[2048,1024]{1,0:T(8,128)} %fusion.33), channel_id=1, replica_groups=mesh['expert'=8,'dp'=32] {'dp'}, use_global_device_ids=true, to_apply=%region_3.4 | all-reduce | flops 2097152 | bytes 12582912 | tf_op jit(solution)/shard_map/psum | solution.py:43
  322.1 0.9 fusion.36
  323.4 2.4 reduce.4
  325.8 0.9 reshape.140
  326.7 4.8 %all-to-all-start = ((bf16[8,2,4096]{2,1,0:T(2,128)(2,1)}), bf16[8,2,4096]{2,1,0:T(2,128)(2,1)S(1)}, u32[]{:S(2)}, u32[]{:S(2)}) async-start(bf16[8,2,4096]{2,1,0:T(2,128)(2,1)} %reshape.140), calls=%async_computation | async-start | bytes 262144 | tf_op jit(solution)/shard_map/all_to_all | solution.py:48
  331.5 5.2 %fusion.23 = bf16[1,448,1024]{2,1,0:T(8,128)(2,1)} fusion(bf16[448,2048]{1,0:T(8,128)(2,1)S(1)} %get-tuple-element.13, bf16[1,1024,2048]{1,2,0:T(8,128)(2,1)} %all-gather.2.cloned.1.call-done), kind=kOutput, calls=%fused_computation.21 | convolution fusion | flops 1879506944 | bytes 6946816 | tf_op jit(solution)/shard_map/esd,efd->efs/dot_general | solution.py:79
  336.7 2.6 reduce_sum.41
  339.3 0.7 reduce_sum.42
  340.7 2.0 multiply_reduce_fusion
  342.7 72.9 %psum.15 = f32[512,2]{0,1:T(2,128)} all-reduce(f32[512,2]{0,1:T(2,128)S(1)} %broadcast_select_fusion), channel_id=1, replica_groups=mesh['expert'=8,'dp'=32] {'dp'}, use_global_device_ids=true, to_apply=%region_6.7 | all-reduce | flops 1024 | bytes 8192 | tf_op jit(solution)/shard_map/psum | solution.py:66
  (43 shorter events, 5.1 us)
Async XLA Ops:
  7.2 105.9 %copy-start = (bf16[1,448,1024]{2,1,0:T(8,128)(2,1)S(1)}, bf16[1,448,1024]{2,1,0:T(8,128)(2,1)}, u32[]{:S(2)}) copy-start(bf16[1,448,1024]{2,1,0:T(8,128)(2,1)} %param.6) | copy-start | bytes 2752516
  7.2 105.9 %all-gather.2.cloned.1.call-start = ((), (), s32[]{:S(2)}) async-start(), calls=%async_computation.2 | async-start | bytes 4325376 | tf_op jit(solution)/shard_map/all_gather | solution.py:77
  12.8 16.6 %copy-start.3 = (bf16[512,64]{0,1:T(8,128)(2,1)S(1)}, bf16[512,64]{0,1:T(8,128)(2,1)}, u32[]{:S(2)}) copy-start(bf16[512,64]{0,1:T(8,128)(2,1)} %param.11) | copy-start | bytes 196612
  13.8 16.2 %copy-start.5 = (f32[1,14,2048]{2,0,1:T(1,128)S(1)}, f32[1,14,2048]{2,0,1:T(1,128)}, u32[]{:S(2)}) copy-start(f32[1,14,2048]{2,0,1:T(1,128)} %param.8) | copy-start | bytes 344068
  14.0 16.4 %copy-start.6 = (s32[512,2]{0,1:T(2,128)S(1)}, s32[512,2]{0,1:T(2,128)}, u32[]{:S(2)}) copy-start(s32[512,2]{0,1:T(2,128)} %param.9) | copy-start | bytes 12292
  117.3 6.5 %copy-start.2 = (f32[1,448,2048]{2,1,0:T(8,128)}, f32[1,448,2048]{2,1,0:T(8,128)S(1)}, u32[]{:S(2)}) copy-start(f32[1,448,2048]{2,1,0:T(8,128)S(1)} %fusion.12) | copy-start | bytes 11010052
  117.4 3.4 copy-start.1
  326.7 13.3 %all-to-all-start = ((bf16[8,2,4096]{2,1,0:T(2,128)(2,1)}), bf16[8,2,4096]{2,1,0:T(2,128)(2,1)S(1)}, u32[]{:S(2)}, u32[]{:S(2)}) async-start(bf16[8,2,4096]{2,1,0:T(2,128)(2,1)} %reshape.140), calls=%async_computation | async-start | bytes 262144 | tf_op jit(solution)/shard_map/all_to_all | solution.py:48
  336.7 4.0 copy-start.4
Sparse Core Ops, SparseCore 0:
  29.4 83.5 all-gather.1
where the time goes:
time: 423 us; the launch traced here: 422 us
  blocking collectives  275 us (65%)
  waiting for transfers between devices  82.7 us (20%)
  matrix products  18.3 us (4%)
  other arithmetic  14.3 us (3%)
  between operations  14.3 us (3%)
  local copies, waits for them, and re-layouts  13.1 us (3%)
  starting transfers between devices  4.84 us (1%)
    psum x1, blocking collectives, on_device(): lax.psum(partial_value.reshape(feature_width, local_experts * slot_total)...  193 us
    all_gather x1, waiting for transfers between devices, on_device(): block_cols = lax.all_gather(arrived, 'dp', axis=2, tiled=True)  82.7 us
    psum x1, blocking collectives, on_device(): gate_grad = lax.psum(gate_partial, 'dp')  72.9 us
    all_to_all x1, blocking collectives, on_device(): lax.all_to_all(outbound, 'expert', split_axis=1, concat_axis=1, tiled=True)  9.39 us
  transfers between devices with their start and end apart: 2, of which 1 were waited for; matrix products, arithmetic and copies ran while one was open for 2% of the time, Pallas kernels for 0%

commit v1 on v0

--- a/solution.py
+++ b/solution.py
@@ -73,7 +73,12 @@
         jnp.bfloat16
     )
     outbound = outbound.reshape(local_experts, slot_total, column_count)
-    arrived = lax.all_to_all(outbound, "expert", split_axis=1, concat_axis=1, tiled=True)
+    arrived = jnp.concatenate(
+        lax.all_to_all(
+            jnp.stack(jnp.split(outbound, lax.axis_size("expert"), axis=1)), "expert", 0, 0
+        ),
+        axis=1,
+    )
     block_cols = lax.all_gather(arrived, "dp", axis=2, tiled=True)
     table_cols = weight_table
     hidden_acc = jnp.einsum(

time: 423 us -> 419 us (level)
  no operation moved by 1% of the time
where the time goes in v1:
time: 419 us
  blocking collectives  275 us (66%)
  waiting for transfers between devices  82.7 us (20%)
  matrix products  18.3 us (4%)
  between operations  14.3 us (3%)
  local copies, waits for them, and re-layouts  11.9 us (3%)
  other arithmetic  11.9 us (3%)
  starting transfers between devices  4.86 us (1%)
    psum x1, blocking collectives, on_device(): lax.psum(partial_value.reshape(feature_width, local_experts * slot_total)...  192 us
    all_gather x1, waiting for transfers between devices, on_device(): block_cols = lax.all_gather(arrived, 'dp', axis=2, tiled=True)  82.7 us
    psum x1, blocking collectives, on_device(): gate_grad = lax.psum(gate_partial, 'dp')  72.9 us
    all_to_all x1, blocking collectives, on_device(): lax.all_to_all(jnp.stack(jnp.split(outbound, lax.axis_size('expert'), axi...  9.39 us
  transfers between devices with their start and end apart: 2, of which 1 were waited for; matrix products, arithmetic and copies ran while one was open for 2% of the time, Pallas kernels for 0%

profile of v1, /device:TPU:8, one launch (start us, length us, event | category | flops | bytes accessed | tf_op | source)
XLA Modules:
  0.0 418.6 jit_solution(11756204937589890643)
XLA Ops:
  7.3 0.9 copy.35
  8.5 2.3 reduce-window.6
  11.8 0.7 broadcast_select_fusion.1
  12.8 0.9 copy.47
  13.9 1.2 fusion.29
  15.3 9.4 %all_to_all.10 = bf16[8,1,128,64]{2,3,1,0:T(8,128)(2,1)S(1)} all-to-all(bf16[8,1,128,64]{2,3,1,0:T(8,128)(2,1)S(1)} %constant_dynamic-update-slice_fusion), channel_id=1, replica_groups=mesh['expert'=8,'dp'=32] {'expert'}, dimensions={0} | all-to-all | bytes 262144 | tf_op jit(solution)/shard_map/all_to_all | solution.py:77
  24.7 0.7 copy_bitcast_fusion
  25.4 0.6 convert_element_type.45
  26.4 82.7 %all-gather.2.cloned.1.call-done = bf16[1,1024,2048]{1,2,0:T(8,128)(2,1)} async-done(((bf16[1,1024,64]{1,2,0:T(8,128)(2,1)}), bf16[1,1024,2048]{1,2,0:T(8,128)(2,1)}) %all-gather.2.cloned.1.call-update) | async-done | bytes 4194320 | tf_op jit(solution)/shard_map/all_gather | solution.py:82
  109.1 4.3 %fusion.12 = f32[1,448,2048]{2,1,0:T(8,128)S(1)} fusion(bf16[1,1024,2048]{1,2,0:T(8,128)(2,1)} %all-gather.2.cloned.1.call-done, bf16[1,448,1024]{2,1,0:T(8,128)(2,1)S(1)} %copy-done), kind=kOutput, calls=%fused_computation.14 | convolution fusion | flops 1879048192 | bytes 8781824 | tf_op jit(solution)/shard_map/efs,esd->efd/dot_general | solution.py:87
  113.9 2.9 copy-done.1
  116.8 3.1 convert_multiply_fusion
  119.9 5.6 %fusion.33 = f32[2048,1024]{1,0:T(8,128)} fusion(bf16[448,2048]{1,0:T(8,128)(2,1)S(1)} %get-tuple-element.13, bf16[1,448,1024]{2,1,0:T(8,128)(2,1)S(1)} %copy-done), kind=kOutput, calls=%fused_computation.25 | convolution fusion | flops 1879048192 | bytes 11141120 | tf_op jit(solution)/shard_map/efs,efd->des/dot_general | solution.py:40
  125.6 192.4 %all-reduce.1 = bf16[2048,1024]{1,0:T(8,128)(2,1)} all-reduce(f32[2048,1024]{1,0:T(8,128)} %fusion.33), channel_id=1, replica_groups=mesh['expert'=8,'dp'=32] {'dp'}, use_global_device_ids=true, to_apply=%region_3.4 | all-reduce | flops 2097152 | bytes 12582912 | tf_op jit(solution)/shard_map/psum | solution.py:43
  318.0 0.9 fusion.36
  319.3 0.5 broadcast.133
  319.8 2.3 reduce.3
  322.1 0.9 reshape.144
  323.0 4.8 %all-to-all-start = ((bf16[8,2,4096]{2,1,0:T(2,128)(2,1)}), bf16[8,2,4096]{2,1,0:T(2,128)(2,1)S(1)}, u32[]{:S(2)}, u32[]{:S(2)}) async-start(bf16[8,2,4096]{2,1,0:T(2,128)(2,1)} %reshape.144), calls=%async_computation | async-start | bytes 262144 | tf_op jit(solution)/shard_map/all_to_all | solution.py:48
  327.8 5.2 %fusion.23 = bf16[1,448,1024]{2,1,0:T(8,128)(2,1)} fusion(bf16[448,2048]{1,0:T(8,128)(2,1)S(1)} %get-tuple-element.13, bf16[1,1024,2048]{1,2,0:T(8,128)(2,1)} %all-gather.2.cloned.1.call-done), kind=kOutput, calls=%fused_computation.21 | convolution fusion | flops 1879506944 | bytes 6946816 | tf_op jit(solution)/shard_map/esd,efd->efs/dot_general | solution.py:84
  333.0 2.6 reduce_sum.41
  335.5 0.7 reduce_sum.42
  336.9 2.0 multiply_reduce_fusion
  338.9 72.9 %psum.15 = f32[512,2]{0,1:T(2,128)} all-reduce(f32[512,2]{0,1:T(2,128)S(1)} %broadcast_select_fusion), channel_id=1, replica_groups=mesh['expert'=8,'dp'=32] {'dp'}, use_global_device_ids=true, to_apply=%region_6.7 | all-reduce | flops 1024 | bytes 8192 | tf_op jit(solution)/shard_map/psum | solution.py:66
  (47 shorter events, 3.8 us)
Async XLA Ops:
  7.2 102.0 %copy-start = (bf16[1,448,1024]{2,1,0:T(8,128)(2,1)S(1)}, bf16[1,448,1024]{2,1,0:T(8,128)(2,1)}, u32[]{:S(2)}) copy-start(bf16[1,448,1024]{2,1,0:T(8,128)(2,1)} %param.6) | copy-start | bytes 2752516
  7.2 19.2 %copy-start.6 = (s32[512,2]{0,1:T(2,128)S(1)}, s32[512,2]{0,1:T(2,128)}, u32[]{:S(2)}) copy-start(s32[512,2]{0,1:T(2,128)} %param.9) | copy-start | bytes 12292
  7.2 18.2 %copy-start.3 = (bf16[512,64]{0,1:T(8,128)(2,1)S(1)}, bf16[512,64]{0,1:T(8,128)(2,1)}, u32[]{:S(2)}) copy-start(bf16[512,64]{0,1:T(8,128)(2,1)} %param.11) | copy-start | bytes 196612
  7.2 18.8 %copy-start.5 = (f32[1,14,2048]{2,0,1:T(1,128)S(1)}, f32[1,14,2048]{2,0,1:T(1,128)}, u32[]{:S(2)}) copy-start(f32[1,14,2048]{2,0,1:T(1,128)} %param.8) | copy-start | bytes 344068
  7.2 101.9 %all-gather.2.cloned.1.call-start = ((), (), s32[]{:S(2)}) async-start(), calls=%async_computation.2 | async-start | bytes 4325376 | tf_op jit(solution)/shard_map/all_gather | solution.py:82
  113.4 6.5 %copy-start.2 = (f32[1,448,2048]{2,1,0:T(8,128)}, f32[1,448,2048]{2,1,0:T(8,128)S(1)}, u32[]{:S(2)}) copy-start(f32[1,448,2048]{2,1,0:T(8,128)S(1)} %fusion.12) | copy-start | bytes 11010052
  113.4 3.4 copy-start.1
  323.0 13.3 %all-to-all-start = ((bf16[8,2,4096]{2,1,0:T(2,128)(2,1)}), bf16[8,2,4096]{2,1,0:T(2,128)(2,1)S(1)}, u32[]{:S(2)}, u32[]{:S(2)}) async-start(bf16[8,2,4096]{2,1,0:T(2,128)(2,1)} %reshape.144), calls=%async_computation | async-start | bytes 262144 | tf_op jit(solution)/shard_map/all_to_all | solution.py:48
  332.9 3.9 copy-start.4
Sparse Core Ops, SparseCore 0:
  25.5 83.5 all-gather.1

commit v2 on v0

--- a/solution.py
+++ b/solution.py
@@ -74,7 +74,9 @@
     )
     outbound = outbound.reshape(local_experts, slot_total, column_count)
     arrived = lax.all_to_all(outbound, "expert", split_axis=1, concat_axis=1, tiled=True)
-    block_cols = lax.all_gather(arrived, "dp", axis=2, tiled=True)
+    block_cols = jnp.concatenate(
+        lax.all_to_all(jnp.stack([arrived] * lax.axis_size("dp")), "dp", 0, 0), axis=2
+    )
     table_cols = weight_table
     hidden_acc = jnp.einsum(
         "esd,efd->efs", block_cols, table_cols, preferred_element_type=jnp.float32

time: 423 us -> 436 us (1.031)
  between operations: 14.3 us -> 0.87 us
  waiting for transfers between devices: 82.7 us -> 95.7 us
  starting transfers between devices: 4.84 us -> 16.3 us
    all_to_all x0 -> x1, waiting for transfers between devices: none -> 95.7 us  [on_device(): lax.all_to_all(jnp.stack([arrived] * lax.axis_size('dp')), 'dp', 0, 0)]
    all_gather x1 -> x0, waiting for transfers between devices: 82.7 us -> none  [on_device(): block_cols = lax.all_gather(arrived, 'dp', axis=2, tiled=True)]
    all_to_all x0 -> x1, starting transfers between devices: none -> 11.6 us  [on_device(): lax.all_to_all(jnp.stack([arrived] * lax.axis_size('dp')), 'dp', 0, 0)]
where the time goes in v2:
time: 436 us; the launch traced here: 435 us
  blocking collectives  275 us (63%)
  waiting for transfers between devices  95.7 us (22%)
  matrix products  18.3 us (4%)
  starting transfers between devices  16.3 us (4%)
  local copies, waits for them, and re-layouts  14.8 us (3%)
  other arithmetic  14.2 us (3%)
    psum x1, blocking collectives, on_device(): lax.psum(partial_value.reshape(feature_width, local_experts * slot_total)...  192 us
    all_to_all x1, waiting for transfers between devices, on_device(): lax.all_to_all(jnp.stack([arrived] * lax.axis_size('dp')), 'dp', 0, 0)  95.7 us
    psum x1, blocking collectives, on_device(): gate_grad = lax.psum(gate_partial, 'dp')  73.5 us
    all_to_all x1, starting transfers between devices, on_device(): lax.all_to_all(jnp.stack([arrived] * lax.axis_size('dp')), 'dp', 0, 0)  11.6 us
    all_to_all x1, blocking collectives, on_device(): lax.all_to_all(outbound, 'expert', split_axis=1, concat_axis=1, tiled=True)  9.39 us
  transfers between devices with their start and end apart: 2, of which 1 were waited for; matrix products, arithmetic and copies ran while one was open for 2% of the time, Pallas kernels for 0%

profile of v2, /device:TPU:8, one launch (start us, length us, event | category | flops | bytes accessed | tf_op | source)
XLA Modules:
  0.0 435.2 jit_solution(16430309691421586035)
XLA Ops:
  0.6 0.9 copy.52
  1.9 2.3 reduce-window.6
  5.2 0.7 broadcast_select_fusion.1
  6.2 0.9 copy.66
  7.3 1.2 fusion.17
  9.4 2.3 reduce.3
  12.0 9.4 %all_to_all.18 = bf16[8,2,4096]{2,1,0:T(2,128)(2,1)S(1)} all-to-all(bf16[8,2,4096]{2,1,0:T(2,128)(2,1)S(1)} %reshape.152), channel_id=1, replica_groups=mesh['expert'=8,'dp'=32] {'expert'}, dimensions={0} | all-to-all | bytes 262144 | tf_op jit(solution)/shard_map/all_to_all | solution.py:76
  22.0 2.5 stack.2
  24.5 11.6 %all-to-all-start.2 = ((bf16[32,1,1024,64]{2,3,1,0:T(8,128)(2,1)}), bf16[32,1,1024,64]{2,3,1,0:T(8,128)(2,1)}, u32[]{:S(2)}, u32[]{:S(2)}) async-start(bf16[32,1,1024,64]{2,3,1,0:T(8,128)(2,1)} %stack.2), calls=%async_computation.2 | async-start | bytes 8388608 | tf_op jit(solution)/shard_map/all_to_all | solution.py:78
  37.1 95.7 %all-to-all-done.2 = bf16[32,1,1024,64]{2,3,1,0:T(8,128)(2,1)} async-done(((bf16[32,1,1024,64]{2,3,1,0:T(8,128)(2,1)}), bf16[32,1,1024,64]{2,3,1,0:T(8,128)(2,1)}, u32[]{:S(2)}, u32[]{:S(2)}) %all-to-all-start.2) | async-done | bytes 4194336 | tf_op jit(solution)/shard_map/all_to_all | solution.py:78
  132.8 4.3 convolution_bitcast_fusion
  137.6 2.9 copy-done.1
  140.5 3.1 convert_multiply_fusion
  143.6 5.6 %fusion.21 = f32[2048,1024]{1,0:T(8,128)} fusion(bf16[448,2048]{1,0:T(8,128)(2,1)S(1)} %get-tuple-element.13, bf16[1,448,1024]{2,1,0:T(8,128)(2,1)S(1)} %copy-done), kind=kOutput, calls=%fused_computation.21 | convolution fusion | flops 1879048192 | bytes 11141120 | tf_op jit(solution)/shard_map/efs,efd->des/dot_general | solution.py:40
  149.2 192.1 %all-reduce.1 = bf16[2048,1024]{1,0:T(8,128)(2,1)} all-reduce(f32[2048,1024]{1,0:T(8,128)} %fusion.21), channel_id=1, replica_groups=mesh['expert'=8,'dp'=32] {'dp'}, use_global_device_ids=true, to_apply=%region_3.4 | all-reduce | flops 2097152 | bytes 12582912 | tf_op jit(solution)/shard_map/psum | solution.py:43
  341.3 0.9 fusion.24
  342.6 2.3 reduce.4
  344.9 0.9 reshape.150
  345.8 4.8 %all-to-all-start = ((bf16[8,2,4096]{2,1,0:T(2,128)(2,1)}), bf16[8,2,4096]{2,1,0:T(2,128)(2,1)S(1)}, u32[]{:S(2)}, u32[]{:S(2)}) async-start(bf16[8,2,4096]{2,1,0:T(2,128)(2,1)} %reshape.150), calls=%async_computation | async-start | bytes 262144 | tf_op jit(solution)/shard_map/all_to_all | solution.py:48
  350.6 5.2 %fusion.13 = bf16[1,448,1024]{2,1,0:T(8,128)(2,1)} fusion(bf16[448,2048]{1,0:T(8,128)(2,1)S(1)} %get-tuple-element.13, bf16[1024,2048]{0,1:T(8,128)(2,1)} %bitcast.13), kind=kOutput, calls=%fused_computation.17 | convolution fusion | flops 1879506944 | bytes 6946816 | tf_op jit(solution)/shard_map/esd,efd->efs/dot_general | solution.py:81
  355.7 2.6 reduce_sum.41
  358.3 0.7 reduce_sum.42
  359.7 2.0 multiply_reduce_fusion
  361.7 73.5 %psum.15 = f32[512,2]{0,1:T(2,128)} all-reduce(f32[512,2]{0,1:T(2,128)S(1)} %broadcast_select_fusion), channel_id=1, replica_groups=mesh['expert'=8,'dp'=32] {'dp'}, use_global_device_ids=true, to_apply=%region_6.7 | all-reduce | flops 1024 | bytes 8192 | tf_op jit(solution)/shard_map/psum | solution.py:66
  (43 shorter events, 6.0 us)
Async XLA Ops:
  0.6 132.2 %copy-start = (bf16[1,448,1024]{2,1,0:T(8,128)(2,1)S(1)}, bf16[1,448,1024]{2,1,0:T(8,128)(2,1)}, u32[]{:S(2)}) copy-start(bf16[1,448,1024]{2,1,0:T(8,128)(2,1)} %param.6) | copy-start | bytes 2752516
  24.5 11.6 %copy-start.3 = (bf16[512,64]{0,1:T(8,128)(2,1)S(1)}, bf16[512,64]{0,1:T(8,128)(2,1)}, u32[]{:S(2)}) copy-start(bf16[512,64]{0,1:T(8,128)(2,1)} %param.11) | copy-start | bytes 196612
  24.5 12.2 %copy-start.5 = (f32[1,14,2048]{2,0,1:T(1,128)S(1)}, f32[1,14,2048]{2,0,1:T(1,128)}, u32[]{:S(2)}) copy-start(f32[1,14,2048]{2,0,1:T(1,128)} %param.8) | copy-start | bytes 344068
  24.5 12.6 %copy-start.6 = (s32[512,2]{0,1:T(2,128)S(1)}, s32[512,2]{0,1:T(2,128)}, u32[]{:S(2)}) copy-start(s32[512,2]{0,1:T(2,128)} %param.9) | copy-start | bytes 12292
  24.5 108.3 %all-to-all-start.2 = ((bf16[32,1,1024,64]{2,3,1,0:T(8,128)(2,1)}), bf16[32,1,1024,64]{2,3,1,0:T(8,128)(2,1)}, u32[]{:S(2)}, u32[]{:S(2)}) async-start(bf16[32,1,1024,64]{2,3,1,0:T(8,128)(2,1)} %stack.2), calls=%async_computation.2 | async-start | bytes 8388608 | tf_op jit(solution)/shard_map/all_to_all | solution.py:78
  137.1 6.5 %copy-start.2 = (f32[1,448,2048]{2,1,0:T(8,128)}, f32[1,448,2048]{2,1,0:T(8,128)S(1)}, u32[]{:S(2)}) copy-start(f32[1,448,2048]{2,1,0:T(8,128)S(1)} %convolution_bitcast_fusion) | copy-start | bytes 11010052
  137.1 3.4 copy-start.1
  345.8 13.2 %all-to-all-start = ((bf16[8,2,4096]{2,1,0:T(2,128)(2,1)}), bf16[8,2,4096]{2,1,0:T(2,128)(2,1)S(1)}, u32[]{:S(2)}, u32[]{:S(2)}) async-start(bf16[8,2,4096]{2,1,0:T(2,128)(2,1)} %reshape.150), calls=%async_computation | async-start | bytes 262144 | tf_op jit(solution)/shard_map/all_to_all | solution.py:48
  355.7 3.9 copy-start.4
